TPU v7x, 128 devices: a whole 4x4x4 slice. The times are simulated.
128 devices in a mesh: row: 16 (over z_lo, x, core), col: 8 (over z_hi, y).
Axes of the slice: x: 4, y: 4, z: 4 (z_hi: 2, z_lo: 2; z = z_hi * 2 + z_lo), core: 2. Of those that a mesh axis runs over, the one named last changes fastest.
Arguments:
- inverse_front: float32 [16384, 16384], P('row', 'col'), may hold values from -0.09375 to 0.09375
- factor: float32 [4096, 1024], P('row'), may hold values from -1.2 to 1.2
- unit_lower: float32 [2, 512, 512], replicated, may hold values from -0.25 to 0.25
- pivot_inverse: float32 [2, 512], replicated, may hold values from 0.5 to 4
- tile_list: int32 [2, 16], replicated, may hold values from 0 to 63, as said below
- tile_valid: int32 [2, 16], replicated, may hold values from 0 to 1, as said below
Outputs:
- inverse_column: float32 [16384, 1024], P('row')
- diagonal_block: float32 [2, 512, 512], replicated
Inputs may be any that keep to these rules, and one draw needn't show every extreme that they name: `tile_list`: each row names 16 different tile rows of the front in increasing order, exactly 1 of them among each aligned group of 4 tile rows, and the last tile row is always among them. `tile_valid`: each row holds at least one 1.
All inputs are finite; a program needn't handle non-finite values.
Results may differ from a plain program's by a relative error of at most 0.0001.
Values sent between devices are 32-bit elements; how exact they have to be, the bound alone decides.
A program may use at most 192 MiB of HBM per device.

v0:
```python
import jax
import jax.numpy as jnp
from jax import lax
from jax.sharding import PartitionSpec as P

B = 256
W = 512
NS = 2
NA = 16


def from_root(block, axis, owner):
    block = jnp.where(lax.axis_index(axis) == owner, block, jnp.zeros_like(block))
    return lax.psum(block, axis)


def inner_left(left, right):
    return lax.dot_general(
        left,
        right,
        (((0,), (0,)), ((), ())),
        precision=lax.Precision.HIGHEST,
        preferred_element_type=jnp.float32,
    )


def shards(inverse_front, factor, unit_lower, pivot_inverse, tile_list, tile_valid):
    row_count = lax.axis_size("row")
    col_count = lax.axis_size("col")
    row_span, col_span = inverse_front.shape
    row_index = lax.axis_index("row")
    col_index = lax.axis_index("col")
    identity = jnp.eye(W, dtype=jnp.float32)
    inverses = [jnp.tril(unit_lower[member], -1) + identity for member in range(NS)]

    def normalize(slab):
        return jnp.concatenate(
            [
                jnp.dot(
                    slab[:, member * W : (member + 1) * W],
                    inverses[member],
                    precision=lax.Precision.HIGHEST,
                    preferred_element_type=jnp.float32,
                )
                for member in range(NS)
            ],
            axis=1,
        )

    normalized = lax.all_gather(normalize(factor), "row", axis=0, tiled=True)
    slot_tiles = normalized.reshape(NA, B, NS, W)

    def place_tiles(first, number):
        global_tile = first + jnp.arange(number, dtype=jnp.int32)
        onehot = (
            (tile_list[:, None, :] == global_tile[None, :, None]) & (tile_valid[:, None, :] > 0)
        ).astype(jnp.float32)
        placed = jnp.einsum("sta,absw->tbsw", onehot, slot_tiles, precision=lax.Precision.HIGHEST)
        return (placed.reshape(number * B, NS * W), jnp.sum(onehot, axis=2))

    row_factor, row_chosen = place_tiles(row_index * (row_span // B), row_span // B)
    col_factor, col_chosen = place_tiles(col_index * (col_span // B), col_span // B)
    row_global = row_index * row_span + jnp.arange(row_span, dtype=jnp.int32)
    col_global = col_index * col_span + jnp.arange(col_span, dtype=jnp.int32)
    lower_part = jnp.where(row_global[:, None] >= col_global[None, :], inverse_front, 0.0)
    lower_prod = jnp.dot(
        lower_part, col_factor, precision=lax.Precision.HIGHEST, preferred_element_type=jnp.float32
    )
    strict = jnp.where(row_global[:, None] > col_global[None, :], inverse_front, 0.0)
    mirror_prod = inner_left(strict, row_factor)
    row_total = lax.psum(lower_prod, "col")
    col_total = lax.psum(mirror_prod, "row")
    grid_ratio = row_count // col_count
    offset = row_index % grid_ratio * row_span
    own_piece = lax.dynamic_slice_in_dim(col_total, offset, row_span, 0)
    mirrored = from_root(own_piece, "col", row_index // grid_ratio)
    keep_rows = jnp.repeat(row_chosen, B, axis=1)
    keep_mask = jnp.repeat(keep_rows.T, W, axis=1)
    column = -(row_total + mirrored) * keep_mask
    base_block = jnp.stack(
        [
            jnp.dot(
                inverses[member].T * pivot_inverse[member][None, :],
                inverses[member],
                precision=lax.Precision.HIGHEST,
                preferred_element_type=jnp.float32,
            )
            for member in range(NS)
        ]
    )
    diag_terms = jnp.stack(
        [
            inner_left(
                row_factor[:, member * W : (member + 1) * W],
                column[:, member * W : (member + 1) * W],
            )
            for member in range(NS)
        ]
    )
    diag_total = lax.psum(diag_terms, "row")
    diagonal_block = base_block - diag_total
    return (column, diagonal_block)


def solution(mesh):
    in_specs = (P("row", "col"), P("row", None), P(), P(), P(), P())
    out_specs = (P("row", None), P())
    return jax.shard_map(shards, mesh=mesh, in_specs=in_specs, out_specs=out_specs, check_vma=False)
```

profile of v0, /device:TPU:1, one launch (start us, length us, event | category | flops | bytes accessed | tf_op | source)
XLA Modules:
  0.0 620.7 jit_solution(13033368712311143179)
XLA Ops:
  7.2 0.0 copy-start.7
  7.2 0.0 all-gather.2.cloned.1.call-start
  7.2 3.3 convolution_bitcast_fusion.1
  10.5 3.3 convolution_bitcast_fusion.2
  13.8 1.0 pad_maximum_fusion.1
  14.8 0.0 all-gather.2.cloned.1.call-update
  14.9 0.0 all-reduce.4.cloned.1.call-start
  15.0 0.0 copy-done.7
  15.0 95.2 %all-gather.2.cloned.1.call-done = f32[4096,1024]{0,1:T(8,128)} async-done(((f32[256,1024]{0,1:T(8,128)}), f32[4096,1024]{0,1:T(8,128)}) %all-gather.2.cloned.1.call-update) | async-done | bytes 16777232 | tf_op jit(solution)/shard_map/all_gather | solution.py:50
  110.2 0.0 copy-start.5
  110.2 11.0 %copy.23 = f32[128,8,16,256]{3,2,1,0:T(8,128)S(1)} copy(f32[128,8,16,256]{3,1,2,0:T(8,128)} %bitcast.71) | data formatting | bytes 33554432
  121.2 0.0 copy-start
  121.2 0.0 copy-done.5
  121.2 6.5 %fusion.57 = f32[2,256,512,4]{1,3,2,0:T(4,128)S(1)} fusion(f32[16,256,2,512]{1,0,3,2:T(8,128)S(1)} %bitcast.67, s32[2,16]{1,0:T(2,128)S(1)} %copy-done.5, pred[2,16]{1,0:T(4,128)(4,1)S(1)} %broadcast_compare_fusion, s32[4]{0:T(128)S(1)} %iota_add_fusion.3), kind=kOutput, calls=%fused_computation.60 | convolution fusion | flops 201326848 | bytes 20971696 | tf_op jit(solution)/shard_map/sta,absw->tbsw/dot_general | solution.py:58
  127.7 0.0 copy-done
  127.7 1.0 copy.25
  128.8 0.0 copy-start.2
  128.8 2.0 copy-done.2
  130.8 57.2 %fusion = f32[2048,1024]{1,0:T(8,128)} fusion(f32[1024,1024]{0,1:T(8,128)S(1)} %bitcast.72, f32[1024,2048]{1,0:T(8,128)} %param.6, s32[2048]{0:T(1024)S(1)} %iota_add_fusion, s32[1024]{0:T(1024)S(1)} %iota_add_fusion.1), kind=kOutput, calls=%fused_computation | convolution fusion | flops 25773998080 | bytes 20983808 | tf_op jit(solution)/shard_map/dot_general | solution.py:18
  188.0 0.0 all-reduce.4.cloned.1.call-update
  188.0 0.0 all-reduce.8.cloned.1.call-start
  188.1 20.3 %copy.14 = f32[16,256,2,512]{3,0,1,2:T(8,128)} copy(f32[16,256,2,512]{1,0,3,2:T(8,128)} %bitcast.68) | data formatting | bytes 33554432 | tf_op jit(solution)/shard_map/reshape | solution.py:51
  208.4 11.9 %convolution_bitcast_fusion = f32[8,256,2,512]{3,0,1,2:T(8,128)} fusion(f32[16,256,2,512]{3,0,1,2:T(8,128)} %copy.14, s32[2,16]{1,0:T(2,128)S(1)} %copy-done.5, s32[8]{0:T(128)S(1)} %iota_add_fusion.4, pred[2,16]{1,0:T(4,128)(4,1)S(1)} %broadcast_compare_fusion), kind=kOutput, calls=%fused_computation.14 | convolution fusion | flops 402653696 | bytes 25166016 | tf_op jit(solution)/shard_map/sta,absw->tbsw/dot_general | solution.py:58
  220.4 10.5 %copy.15 = f32[8,256,2,512]{1,0,3,2:T(8,128)} copy(f32[8,256,2,512]{3,0,1,2:T(8,128)} %convolution_bitcast_fusion) | data formatting | bytes 16777216 | tf_op jit(solution)/shard_map/sta,absw->tbsw/transpose | solution.py:58
  230.8 10.9 %copy.24 = f32[128,8,8,256]{3,1,2,0:T(8,128)} copy(f32[128,8,8,256]{3,2,1,0:T(8,128)} %bitcast.69) | data formatting | bytes 16777216
  241.8 87.7 %all-reduce.4.cloned.1.call-done = f32[2048,1024]{1,0:T(8,128)} async-done(((f32[2048,1024]{1,0:T(8,128)}), f32[2048,1024]{1,0:T(8,128)}) %all-reduce.4.cloned.1.call-update) | async-done | bytes 8388624 | tf_op jit(solution)/shard_map/psum | solution.py:72
  329.5 33.9 %select_add_fusion = f32[1024,1024]{1,0:T(8,128)} fusion(f32[2048,1024]{1,0:T(8,128)} %all-reduce.4.cloned.1.call-done, s32[]{:T(128)S(6)} %select_n.43, pred[]{:T(512)S(6)} %eq.40, f32[2048,1024]{0,1:T(8,128)} %bitcast.77, f32[1024,2048]{1,0:T(8,128)} %param.6, s32[2048]{0:T(1024)S(1)} %iota_add_fusion, s32[1024]{0:T(1024)S(1)} %iota_add_fusion.1), kind=kOutput, calls=%fused_computation.7 | convolution fusion | flops 25776095232 | bytes 25178116 | tf_op jit(solution)/shard_map/dot_general | solution.py:66
  363.4 0.0 all-reduce.8.cloned.1.call-update
  363.4 0.2 all-reduce.6.cloned.1.call-start
  363.6 0.2 convert_reduce_fusion
  363.8 0.1 copy.17
  363.9 1.4 broadcast_in_dim.33
  365.3 3.0 copy.26
  368.3 106.8 %all-reduce.8.cloned.1.call-done = f32[1024,1024]{1,0:T(8,128)} async-done(((f32[1024,1024]{1,0:T(8,128)}), f32[1024,1024]{1,0:T(8,128)}) %all-reduce.8.cloned.1.call-update) | async-done | bytes 4194320 | tf_op jit(solution)/shard_map/psum | solution.py:71
  475.1 0.0 copy-start.3
  475.1 4.6 negate_multiply_fusion
  479.7 0.1 copy-done.3
  479.8 0.0 copy-start.1
  479.8 3.5 fusion.35
  483.3 3.5 fusion.30
  486.8 0.0 copy-done.1
  486.8 0.0 copy-start.6
  486.8 0.0 copy-start.4
  486.8 1.5 pad_maximum_fusion
  488.3 0.0 all-reduce.6.cloned.1.call-update
  488.3 0.0 copy-done.6
  488.4 0.8 copy-done.4
  489.2 2.3 fusion.27
  491.5 3.3 fusion.24
  494.8 115.6 %all-reduce.6.cloned.1.call-done = f32[2,512,512]{2,1,0:T(8,128)} async-done(((f32[2,512,512]{2,1,0:T(8,128)}), f32[2,512,512]{2,1,0:T(8,128)}) %all-reduce.6.cloned.1.call-update) | async-done | bytes 2097168 | tf_op jit(solution)/shard_map/psum | solution.py:100
  610.4 3.7 maximum_subtract_fusion
  (8 shorter events, 0.1 us)
Async XLA Ops:
  7.2 7.8 %copy-start.7 = (s32[2,16]{1,0:T(2,128)S(1)}, s32[2,16]{1,0:T(2,128)}, u32[]{:S(2)}) copy-start(s32[2,16]{1,0:T(2,128)} %param.11) | copy-start | bytes 388
  7.2 103.1 %all-gather.2.cloned.1.call-start = ((), (), s32[]{:S(2)}) async-start(), calls=%async_computation | async-start | bytes 17825792 | tf_op jit(solution)/shard_map/all_gather | solution.py:50
  14.9 314.6 %all-reduce.4.cloned.1.call-start = ((), (), s32[]{:S(2)}) async-start(), calls=%async_computation.1 | async-start | bytes 16777216 | tf_op jit(solution)/shard_map/psum | solution.py:72
  110.2 11.0 %copy-start.5 = (s32[2,16]{1,0:T(2,128)S(1)}, s32[2,16]{1,0:T(2,128)}, u32[]{:S(2)}) copy-start(s32[2,16]{1,0:T(2,128)} %param.10) | copy-start | bytes 388
  121.2 6.5 %copy-start = (f32[128,8,16,256]{3,2,1,0:T(8,128)}, f32[128,8,16,256]{3,2,1,0:T(8,128)S(1)}, u32[]{:S(2)}) copy-start(f32[128,8,16,256]{3,2,1,0:T(8,128)S(1)} %copy.23) | copy-start | bytes 50331652
  128.8 2.1 copy-start.2
  188.0 287.1 %all-reduce.8.cloned.1.call-start = ((), (), s32[]{:S(2)}) async-start(), calls=%async_computation.3 | async-start | bytes 8388608 | tf_op jit(solution)/shard_map/psum | solution.py:71
  363.4 247.0 %all-reduce.6.cloned.1.call-start = ((), (), s32[]{:S(2)}) async-start(), calls=%async_computation.2 | async-start | bytes 4194304 | tf_op jit(solution)/shard_map/psum | solution.py:100
  475.1 4.6 copy-start.3
  479.8 7.0 %copy-start.1 = (f32[1024,1024]{1,0:T(8,128)}, f32[1024,1024]{1,0:T(8,128)S(1)}, u32[]{:S(2)}) copy-start(f32[1024,1024]{1,0:T(8,128)S(1)} %negate_multiply_fusion) | copy-start | bytes 12582916
  486.8 1.5 copy-start.6
  486.8 2.4 copy-start.4
Sparse Core Ops, SparseCore 0:
  15.0 95.2 all-gather.1
  188.1 141.3 all-reduce.3
  363.5 111.5 all-reduce.7
  488.5 121.8 all-reduce.5
where the time goes:
time: 629 us; the launch traced here: 621 us
  waiting for transfers between devices  405 us (64%)
  matrix products  129 us (21%)
  local copies, waits for them, and re-layouts  61.2 us (10%)
  between operations  14.2 us (2%)
  other arithmetic  10.9 us (2%)
    psum x1, waiting for transfers between devices, shards(): diag_total = lax.psum(diag_terms, 'row')  116 us
    psum x1, waiting for transfers between devices, shards(): row_total = lax.psum(lower_prod, 'col')  107 us
    all_gather x1, waiting for transfers between devices, shards(): normalized = lax.all_gather(normalize(factor), 'row', axis=0, tiled=True)  95.2 us
    psum x1, waiting for transfers between devices, shards(): col_total = lax.psum(mirror_prod, 'row')  87.7 us
    dot_general x3, matrix products, inner_left(): lax.dot_general(left, right, (((0,), (0,)), ((), ())), precision=lax.Prec...  64.2 us
    dot_general x1, matrix products, shards(): jnp.dot(lower_part, col_factor, precision=lax.Precision.HIGHEST, preferre...  33.9 us
    unnamed x20, local copies, waits for them, and re-layouts  28.9 us
    reshape x1, local copies, waits for them, and re-layouts, shards(): slot_tiles = normalized.reshape(NA, B, NS, W)  20.3 us
  transfers between devices with their start and end apart: 4, of which 4 were waited for; matrix products, arithmetic and copies ran while one was open for 10% of the time, Pallas kernels for 0%

commit v1 on v0

--- a/solution.py
+++ b/solution.py
@@ -25,6 +25,18 @@
 
 
 def shards(inverse_front, factor, unit_lower, pivot_inverse, tile_list, tile_valid):
+
+    def launch_the_outputs(local, which_axis):
+        return jnp.concatenate(
+            lax.all_to_all(
+                jnp.stack([local for _ in range(lax.axis_size(which_axis))]),
+                which_axis,
+                split_axis=0,
+                concat_axis=0,
+            ),
+            0,
+        )
+
     row_count = lax.axis_size("row")
     col_count = lax.axis_size("col")
     row_span, col_span = inverse_front.shape
@@ -47,7 +59,7 @@
             axis=1,
         )
 
-    normalized = lax.all_gather(normalize(factor), "row", axis=0, tiled=True)
+    normalized = launch_the_outputs(normalize(factor), "row")
     slot_tiles = normalized.reshape(NA, B, NS, W)
 
     def place_tiles(first, number):

time: 629 us -> 758 us (1.21)
  waiting for transfers between devices: 405 us -> 556 us
  matrix products: 129 us -> 105 us
    all_to_all x0 -> x1, waiting for transfers between devices: none -> 224 us  [launch_the_outputs(): lax.all_to_all(jnp.stack([local for _ in range(lax.axis_size(which_axis))...]
    all_gather x1 -> x0, waiting for transfers between devices: 95.2 us -> none  [shards(): normalized = lax.all_gather(normalize(factor), 'row', axis=0, tiled=True)]
    another operation x0 -> x2, local copies, waits for them, and re-layouts: none -> 27.6 us  [the longest x1 20.3 us: shards(): slot_tiles = normalized.reshape(NA, B, NS, W)]
    dot_general x3, matrix products: 64.2 us -> 37.3 us  [inner_left(): lax.dot_general(left, right, (((0,), (0,)), ((), ())), precision=lax.Prec...]
    psum x1, waiting for transfers between devices: 87.7 us -> 110 us  [shards(): col_total = lax.psum(mirror_prod, 'row')]
    reshape x1 -> x0, local copies, waits for them, and re-layouts: 20.3 us -> none  [shards(): slot_tiles = normalized.reshape(NA, B, NS, W)]
    unnamed x20 -> x21, local copies, waits for them, and re-layouts: 28.9 us -> 17.6 us
  transfers between devices with their start and end apart: 4 -> 4, of which waited for: 4 -> 4; matrix products, arithmetic and copies ran while one was open for 10% -> 6% of each run, Pallas kernels for 0% -> 0%
where the time goes in v1:
time: 758 us; the launch traced here: 753 us
  waiting for transfers between devices  556 us (73%)
  matrix products  105 us (14%)
  local copies, waits for them, and re-layouts  60.7 us (8%)
  between operations  14.2 us (2%)
  other arithmetic  9.98 us (1%)
  starting transfers between devices  7.58 us (1%)
    all_to_all x1, waiting for transfers between devices, launch_the_outputs(): lax.all_to_all(jnp.stack([local for _ in range(lax.axis_size(which_axis))...  224 us
    psum x1, waiting for transfers between devices, shards(): diag_total = lax.psum(diag_terms, 'row')  115 us
    psum x1, waiting for transfers between devices, shards(): col_total = lax.psum(mirror_prod, 'row')  110 us
    psum x1, waiting for transfers between devices, shards(): row_total = lax.psum(lower_prod, 'col')  107 us
    dot_general x3, matrix products, inner_left(): lax.dot_general(left, right, (((0,), (0,)), ((), ())), precision=lax.Prec...  37.3 us
    dot_general x1, matrix products, shards(): jnp.dot(lower_part, col_factor, precision=lax.Precision.HIGHEST, preferre...  33.9 us
    dot_general x2, matrix products, place_tiles(): jnp.einsum('sta,absw->tbsw', onehot, slot_tiles, precision=lax.Precision....  21.5 us
    another operation x1, local copies, waits for them, and re-layouts, shards(): slot_tiles = normalized.reshape(NA, B, NS, W)  20.3 us
  transfers between devices with their start and end apart: 4, of which 4 were waited for; matrix products, arithmetic and copies ran while one was open for 6% of the time, Pallas kernels for 0%

profile of v1, /device:TPU:1, one launch (start us, length us, event | category | flops | bytes accessed | tf_op | source)
XLA Modules:
  0.0 753.2 jit_solution(11226185220218540625)
XLA Ops:
  7.2 3.3 convolution_bitcast_fusion.2
  10.5 3.3 convolution_bitcast_fusion.3
  13.7 0.1 pad_maximum_fusion.1
  13.8 7.4 stack.14
  21.2 0.0 copy-start.6
  21.2 7.3 all-to-all-start
  28.5 0.2 all-reduce.4.cloned.1.call-start
  28.7 0.0 copy-done.6
  28.8 224.0 %all-to-all-done = f32[16,256,1024]{1,2,0:T(8,128)} async-done(((f32[16,256,1024]{1,2,0:T(8,128)}), f32[16,256,1024]{1,2,0:T(8,128)}, u32[]{:S(2)}, u32[]{:S(2)}) %all-to-all-start) | async-done | bytes 16777248 | tf_op jit(solution)/shard_map/all_to_all | solution.py:31
  252.8 0.0 copy-start.4
  252.8 20.3 %copy.13 = f32[16,256,2,512]{3,0,1,2:T(8,128)} copy(f32[16,256,2,512]{1,3,2,0:T(8,128)} %bitcast.4) | data formatting | bytes 33554432 | tf_op jit(solution)/shard_map/reshape;reshape | solution.py:63
  273.1 0.0 copy-done.4
  273.1 9.7 %convolution_bitcast_fusion.1 = f32[4,256,2,512]{3,0,1,2:T(4,128)S(1)} fusion(f32[16,256,2,512]{3,0,1,2:T(8,128)} %copy.13, s32[2,16]{1,0:T(2,128)S(1)} %copy-done.4, pred[2,16]{1,0:T(4,128)(4,1)S(1)} %broadcast_compare_fusion, s32[4]{0:T(128)S(1)} %iota_add_fusion.3), kind=kOutput, calls=%fused_computation.15 | convolution fusion | flops 201326848 | bytes 20971696 | tf_op jit(solution)/shard_map/sta,absw->tbsw/dot_general | solution.py:70
  282.8 0.0 slice-start
  282.8 3.2 copy.16
  286.0 0.0 slice-start.1
  286.0 1.0 copy.21
  287.1 0.0 copy-start.1
  287.1 1.9 copy-done.1
  289.0 0.0 slice-done
  289.0 0.0 slice-done.1
  289.0 30.1 %fusion = f32[2048,1024]{1,0:T(8,128)} fusion(f32[1024,1024]{1,0:T(8,128)S(1)} %bitcast.64, f32[1024,2048]{1,0:T(8,128)S(1)} %bitcast.74, s32[2048]{0:T(1024)S(1)} %iota_add_fusion, s32[1024]{0:T(1024)S(1)} %iota_add_fusion.1), kind=kOutput, calls=%fused_computation | convolution fusion | flops 25773998080 | bytes 20983808 | tf_op jit(solution)/shard_map/dot_general | solution.py:18
  319.1 0.0 all-reduce.4.cloned.1.call-update
  319.2 0.0 all-reduce.8.cloned.1.call-start
  319.2 11.8 %convolution_bitcast_fusion = f32[8,256,2,512]{3,0,1,2:T(8,128)} fusion(f32[16,256,2,512]{3,0,1,2:T(8,128)} %copy.13, s32[2,16]{1,0:T(2,128)S(1)} %copy-done.4, s32[8]{0:T(128)S(1)} %iota_add_fusion.4, pred[2,16]{1,0:T(4,128)(4,1)S(1)} %broadcast_compare_fusion), kind=kOutput, calls=%fused_computation.14 | convolution fusion | flops 402653696 | bytes 25166016 | tf_op jit(solution)/shard_map/sta,absw->tbsw/dot_general | solution.py:70
  331.1 10.5 %copy.14 = f32[8,256,2,512]{1,0,3,2:T(8,128)} copy(f32[8,256,2,512]{3,0,1,2:T(8,128)} %convolution_bitcast_fusion) | data formatting | bytes 16777216 | tf_op jit(solution)/shard_map/sta,absw->tbsw/transpose | solution.py:70
  341.5 10.7 %copy.20 = f32[128,8,8,256]{3,1,2,0:T(8,128)} copy(f32[128,8,8,256]{3,2,1,0:T(8,128)} %bitcast.62) | data formatting | bytes 16777216
  352.3 109.6 %all-reduce.4.cloned.1.call-done = f32[2048,1024]{1,0:T(8,128)} async-done(((f32[2048,1024]{1,0:T(8,128)}), f32[2048,1024]{1,0:T(8,128)}) %all-reduce.4.cloned.1.call-update) | async-done | bytes 8388624 | tf_op jit(solution)/shard_map/psum | solution.py:84
  461.8 33.9 %select_add_fusion = f32[1024,1024]{1,0:T(8,128)} fusion(f32[2048,1024]{1,0:T(8,128)} %all-reduce.4.cloned.1.call-done, s32[]{:T(128)S(6)} %select_n.43, pred[]{:T(512)S(6)} %eq.40, f32[2048,1024]{0,1:T(8,128)} %bitcast.69, f32[1024,2048]{1,0:T(8,128)} %param.6, s32[2048]{0:T(1024)S(1)} %iota_add_fusion, s32[1024]{0:T(1024)S(1)} %iota_add_fusion.1), kind=kOutput, calls=%fused_computation.7 | convolution fusion | flops 25776095232 | bytes 25178116 | tf_op jit(solution)/shard_map/dot_general | solution.py:78
  495.7 0.0 all-reduce.8.cloned.1.call-update
  495.7 0.0 all-reduce.6.cloned.1.call-start
  495.8 0.2 convert_reduce_fusion
  495.9 0.1 copy.17
  496.1 1.6 broadcast_in_dim.33
  497.6 3.0 copy.22
  500.6 106.7 %all-reduce.8.cloned.1.call-done = f32[1024,1024]{1,0:T(8,128)} async-done(((f32[1024,1024]{1,0:T(8,128)}), f32[1024,1024]{1,0:T(8,128)}) %all-reduce.8.cloned.1.call-update) | async-done | bytes 4194320 | tf_op jit(solution)/shard_map/psum | solution.py:83
  607.4 0.0 copy-start.2
  607.4 4.6 negate_multiply_fusion
  612.0 0.1 copy-done.2
  612.0 0.0 copy-start
  612.0 3.6 fusion.30
  615.6 3.6 fusion.35
  619.2 0.0 copy-done
  619.2 0.0 copy-start.5
  619.2 0.0 copy-start.3
  619.3 1.5 pad_maximum_fusion
  620.7 0.0 all-reduce.6.cloned.1.call-update
  620.8 0.0 copy-done.5
  620.8 0.8 copy-done.3
  621.6 2.3 fusion.24
  623.9 3.5 fusion.27
  627.4 115.3 %all-reduce.6.cloned.1.call-done = f32[2,512,512]{2,1,0:T(8,128)} async-done(((f32[2,512,512]{2,1,0:T(8,128)}), f32[2,512,512]{2,1,0:T(8,128)}) %all-reduce.6.cloned.1.call-update) | async-done | bytes 2097168 | tf_op jit(solution)/shard_map/psum | solution.py:112
  742.8 3.7 maximum_subtract_fusion
  (9 shorter events, 0.1 us)
Async XLA Ops:
  21.2 7.6 %copy-start.6 = (s32[2,16]{1,0:T(2,128)S(1)}, s32[2,16]{1,0:T(2,128)}, u32[]{:S(2)}) copy-start(s32[2,16]{1,0:T(2,128)} %param.11) | copy-start | bytes 388
  21.2 231.6 %all-to-all-start = ((f32[16,256,1024]{1,2,0:T(8,128)}), f32[16,256,1024]{1,2,0:T(8,128)}, u32[]{:S(2)}, u32[]{:S(2)}) async-start(f32[16,256,1024]{1,2,0:T(8,128)} %stack.14), calls=%async_computation | async-start | bytes 33554432 | tf_op jit(solution)/shard_map/all_to_all | solution.py:31
  28.5 433.3 %all-reduce.4.cloned.1.call-start = ((), (), s32[]{:S(2)}) async-start(), calls=%async_computation.1 | async-start | bytes 16777216 | tf_op jit(solution)/shard_map/psum | solution.py:84
  252.8 20.3 %copy-start.4 = (s32[2,16]{1,0:T(2,128)S(1)}, s32[2,16]{1,0:T(2,128)}, u32[]{:S(2)}) copy-start(s32[2,16]{1,0:T(2,128)} %param.10) | copy-start | bytes 388
  282.8 6.3 slice-start
  286.0 3.0 slice-start.1
  287.1 2.0 copy-start.1
  319.2 288.2 %all-reduce.8.cloned.1.call-start = ((), (), s32[]{:S(2)}) async-start(), calls=%async_computation.3 | async-start | bytes 8388608 | tf_op jit(solution)/shard_map/psum | solution.py:83
  495.7 247.1 %all-reduce.6.cloned.1.call-start = ((), (), s32[]{:S(2)}) async-start(), calls=%async_computation.2 | async-start | bytes 4194304 | tf_op jit(solution)/shard_map/psum | solution.py:112
  607.4 4.6 copy-start.2
  612.0 7.2 copy-start
  619.2 1.5 copy-start.5
  619.2 2.4 copy-start.3
Sparse Core Ops, SparseCore 0:
  319.3 142.4 all-reduce.3
  495.8 111.5 all-reduce.7
  620.9 121.8 all-reduce.5
